TPU v7x, 32 devices: a whole 2x2x4 slice. The times are simulated.
32 devices in a mesh: src: 4 (over y, x), dst: 8 (over z, core).
Axes of the slice: x: 2, y: 2, z: 4, core: 2. Of those that a mesh axis runs over, the one named last changes fastest.
Arguments:
- transition: bfloat16 [32768, 32768], P('src', 'dst'), may hold values from -0.046875 to 0.046875
- emit_cols: bfloat16 [16, 32768], P(None, 'dst'), may hold values from 0.25 to 4
- token_ids: int32 [48, 4], replicated, may hold values from 0 to 15
- alpha_start: bfloat16 [48, 32768], P(None, 'src'), may hold values from -6 to 6
- beta_end: bfloat16 [48, 32768], P(None, 'dst'), may hold values from -6 to 6
- inverse_likelihood: float32 [48], replicated, may hold values from 5 to 80
Outputs:
- counts: float32 [8192, 8192], P('src', 'dst')
Inputs may be any that keep to these rules, and one draw needn't show every extreme that they name: `token_ids`: each id selects one of the 16 supplied emission columns.
All inputs are finite; a program needn't handle non-finite values.
Results may differ from a plain program's by a relative error of at most 0.024.
Values may be sent and summed in bfloat16 or wider, within the bound.
No kernel may reach another device: no remote copies, remote signals or barrier semaphores. Data moves between devices by JAX's collectives and lax.ppermute only.
A program may use at most 128 MiB of HBM per device.

v0:
```python
import jax
import jax.numpy as jnp
from jax import lax
from jax.sharding import PartitionSpec as P

scaling = 0.75


def per_device(transition, emit_cols, token_ids, alpha_start, beta_end, inverse_likelihood):
    src_tile = transition.shape[0]
    dst_tile = transition.shape[1]
    src_count = lax.axis_size("src")
    dst_count = lax.axis_size("dst")
    tile_ratio = dst_count // src_count
    row_place = lax.axis_index("src")
    col_place = lax.axis_index("dst")
    seq_rows = alpha_start.shape[0]
    column_codes = lax.broadcasted_iota(jnp.int32, (1, emit_cols.shape[0]), 1)

    def emitted(position):
        selector = (token_ids[:, position : position + 1] == column_codes).astype(jnp.bfloat16)
        return jnp.dot(selector, emit_cols, preferred_element_type=jnp.float32)

    def forward(current, position):
        partial_value = jnp.dot(current, transition, preferred_element_type=jnp.float32)
        slice_width = dst_tile // src_count
        shared = lax.psum_scatter(
            partial_value.astype(jnp.bfloat16), "src", scatter_dimension=1, tiled=True
        ).astype(jnp.float32)
        emit_slice = lax.dynamic_slice_in_dim(
            emitted(position), row_place * slice_width, slice_width, 1
        )
        advanced = (scaling * emit_slice * shared).astype(jnp.bfloat16)
        spread = lax.all_gather(advanced, "dst", axis=1, tiled=True)
        shaped = spread.reshape(seq_rows, src_count, tile_ratio, 1, slice_width)
        regrouped = lax.all_to_all(shaped, "src", split_axis=1, concat_axis=3, tiled=True)
        return regrouped.reshape(seq_rows, src_tile)

    def backward(carried, position):
        partial_value = lax.dot_general(
            carried, transition, (((1,), (1,)), ((), ())), preferred_element_type=jnp.float32
        )
        slice_width = src_tile // dst_count
        shared = lax.psum_scatter(partial_value, "dst", scatter_dimension=1, tiled=True).astype(
            jnp.bfloat16
        )
        spread = lax.all_gather(shared, "src", axis=1, tiled=True)
        tiles = spread.reshape(seq_rows, src_count, 1, slice_width)
        outgoing = jnp.broadcast_to(tiles, (seq_rows, src_count, tile_ratio, slice_width)).reshape(
            seq_rows, dst_count, 1, slice_width
        )
        regrouped = lax.all_to_all(outgoing, "dst", split_axis=1, concat_axis=2, tiled=True)
        whole_tile = regrouped.reshape(seq_rows, src_tile)
        own_part = lax.dynamic_slice_in_dim(
            whole_tile, col_place % tile_ratio * dst_tile, dst_tile, 1
        )
        return (scaling * emitted(position) * own_part.astype(jnp.float32)).astype(jnp.bfloat16)

    alpha_one = forward(alpha_start, 0)
    alpha_two = forward(alpha_one, 1)
    message_four = (scaling * emitted(3) * beta_end.astype(jnp.float32)).astype(jnp.bfloat16)
    message_three = backward(message_four, 2)
    message_two = backward(message_three, 1)
    quarter_rows = src_tile // 4
    quarter_width = dst_tile // 4
    weights = inverse_likelihood[:, None]
    outer_sum = jnp.zeros((quarter_rows, quarter_width), jnp.float32)
    for alpha_rows, message in ((alpha_one, message_two), (alpha_two, message_three)):
        weighted = (weights * message[:, :quarter_width].astype(jnp.float32)).astype(jnp.bfloat16)
        outer_sum = outer_sum + lax.dot_general(
            alpha_rows[:, :quarter_rows],
            weighted,
            (((0,), (0,)), ((), ())),
            preferred_element_type=jnp.float32,
        )
    return transition[:quarter_rows, :quarter_width].astype(jnp.float32) * outer_sum


def solution(mesh):
    in_specs = (P("src", "dst"), P(None, "dst"), P(), P(None, "src"), P(None, "dst"), P())
    out_specs = P("src", "dst")
    return jax.shard_map(
        per_device, mesh=mesh, in_specs=in_specs, out_specs=out_specs, check_vma=False
    )
```

profile of v0, /device:TPU:0, one launch (start us, length us, event | category | flops | bytes accessed | tf_op | source)
XLA Modules:
  0.0 261.0 jit_solution(8276515694606811173)
XLA Ops:
  6.5 0.0 reduce-scatter.5.cloned.1.call-start
  6.6 1.1 copy-done
  7.7 24.1 %convolution_convert_fusion.1 = bf16[48,4096]{1,0:T(8,128)(2,1)} fusion(bf16[48,8192]{1,0:T(8,128)(2,1)S(1)} %copy-done, bf16[8192,4096]{1,0:T(8,128)(2,1)} %param.6), kind=kOutput, calls=%fused_computation.8 | convolution fusion | flops 3221422080 | bytes 68288512 | tf_op jit(solution)/shard_map/dot_general | solution.py:25
  31.8 0.0 reduce-scatter.5.cloned.1.call-update
  31.8 0.0 reduce-scatter.7.cloned.1.call-start
  31.9 30.0 %fusion.4 = f32[48,8192]{1,0:T(8,128)} fusion(bf16[8192,4096]{1,0:T(8,128)(2,1)} %param.6, bf16[16,4096]{1,0:T(8,128)(2,1)S(1)} %copy-done.1, bf16[48,4096]{1,0:T(8,128)(2,1)S(1)} %copy-done.2, s32[48]{0:T(128)S(1)} %get-tuple-element.8), kind=kOutput, calls=%fused_computation.9 | convolution fusion | flops 3228304128 | bytes 69206208 | tf_op jit(solution)/shard_map/dot_general | solution.py:40
  62.0 0.0 reduce-scatter.7.cloned.1.call-update
  62.0 0.3 fusion.18
  62.3 0.0 reduce-scatter.5.cloned.1.call-done
  62.3 0.9 multiply_convert_fusion.3
  63.3 20.5 %all_gather.12 = bf16[48,8192]{1,0:T(8,128)(2,1)S(1)} all-gather(bf16[48,1024]{1,0:T(8,128)(2,1)S(1)} %multiply_convert_fusion.3), channel_id=1, replica_groups=mesh['src'=4,'dst'=8] {'dst'}, dimensions={1}, use_global_device_ids=true | all-gather | bytes 884736 | tf_op jit(solution)/shard_map/all_gather | solution.py:34
  83.8 0.6 reshape.39
  84.4 1.5 copy.9
  85.8 3.8 %all-to-all-start = ((bf16[48,4,2,1,1024]{4,2,0,3,1:T(2,128)(2,1)}), bf16[48,4,2,1,1024]{4,2,0,3,1:T(2,128)(2,1)S(1)}, u32[]{:S(2)}, u32[]{:S(2)}) async-start(bf16[48,4,2,1,1024]{4,2,0,3,1:T(2,128)(2,1)} %copy.9), calls=%async_computation.1 | async-start | bytes 1572864 | tf_op jit(solution)/shard_map/all_to_all | solution.py:36
  89.6 11.3 %all-to-all-done = bf16[48,4,2,1,1024]{4,2,0,3,1:T(2,128)(2,1)S(1)} async-done(((bf16[48,4,2,1,1024]{4,2,0,3,1:T(2,128)(2,1)}), bf16[48,4,2,1,1024]{4,2,0,3,1:T(2,128)(2,1)S(1)}, u32[]{:S(2)}, u32[]{:S(2)}) %all-to-all-start) | async-done | bytes 786464 | tf_op jit(solution)/shard_map/all_to_all | solution.py:36
  100.9 0.6 copy.10
  101.5 0.6 reshape.40
  102.1 0.0 reduce-scatter.7.cloned.1.call-done
  102.1 0.9 convert_element_type.68
  103.1 9.9 %all_gather.13 = bf16[48,4096]{1,0:T(8,128)(2,1)S(1)} all-gather(bf16[48,1024]{1,0:T(8,128)(2,1)S(1)} %convert_element_type.68), channel_id=1, replica_groups=mesh['src'=4,'dst'=8] {'src'}, dimensions={1}, use_global_device_ids=true | all-gather | bytes 491520 | tf_op jit(solution)/shard_map/all_gather | solution.py:47
  113.0 1.0 broadcast_in_dim.16
  114.0 3.9 %all-to-all-start.1 = ((bf16[48,8,1,1024]{3,0,2,1:T(8,128)(2,1)}), bf16[48,8,1,1024]{3,0,2,1:T(8,128)(2,1)S(1)}, u32[]{:S(2)}, u32[]{:S(2)}) async-start(bf16[48,8,1,1024]{3,0,2,1:T(8,128)(2,1)} %bitcast.6), calls=%async_computation.3 | async-start | bytes 1572864 | tf_op jit(solution)/shard_map/all_to_all | solution.py:52
  117.9 0.0 reduce-scatter.11.cloned.1.call-start
  117.9 24.1 %convolution_convert_fusion = bf16[48,4096]{1,0:T(8,128)(2,1)} fusion(bf16[48,8192]{1,0:T(8,128)(2,1)S(1)} %reshape.40, bf16[8192,4096]{1,0:T(8,128)(2,1)} %param.6), kind=kOutput, calls=%fused_computation.7 | convolution fusion | flops 3221422080 | bytes 68288512 | tf_op jit(solution)/shard_map/dot_general | solution.py:25
  142.1 0.0 reduce-scatter.11.cloned.1.call-update
  142.1 0.2 reduce-scatter.9.cloned.1.call-start
  142.3 0.0 all-to-all-done.1
  142.3 0.1 copy.19
  142.4 0.3 fusion.2
  142.7 29.5 %fusion.28 = f32[48,8192]{1,0:T(8,128)} fusion(bf16[48,4096]{1,0:T(8,128)(2,1)S(1)} %fusion.2, bf16[8192,4096]{1,0:T(8,128)(2,1)} %param.6), kind=kOutput, calls=%fused_computation.46 | convolution fusion | flops 3221225472 | bytes 69074944 | tf_op jit(solution)/shard_map/dot_general | solution.py:40
  172.2 0.0 reduce-scatter.9.cloned.1.call-update
  172.2 1.2 fusion.19
  173.5 1.0 multiply_convert_fusion.1
  174.5 20.2 %all_gather.15 = bf16[48,8192]{1,0:T(8,128)(2,1)S(1)} all-gather(bf16[48,1024]{1,0:T(8,128)(2,1)S(1)} %multiply_convert_fusion.1), channel_id=1, replica_groups=mesh['src'=4,'dst'=8] {'dst'}, dimensions={1}, use_global_device_ids=true | all-gather | bytes 884736 | tf_op jit(solution)/shard_map/all_gather | solution.py:34
  194.7 0.6 reshape.45
  195.2 1.5 copy.15
  196.7 3.5 %all-to-all-start.3 = ((bf16[48,4,2,1,1024]{4,2,0,3,1:T(2,128)(2,1)}), bf16[48,4,2,1,1024]{4,2,0,3,1:T(2,128)(2,1)S(1)}, u32[]{:S(2)}, u32[]{:S(2)}) async-start(bf16[48,4,2,1,1024]{4,2,0,3,1:T(2,128)(2,1)} %copy.15), calls=%async_computation.7 | async-start | bytes 1572864 | tf_op jit(solution)/shard_map/all_to_all | solution.py:36
  200.2 9.3 %reduce-scatter.9.cloned.1.call-done = f32[48,1024]{1,0:T(8,128)} async-done(((f32[48,8192]{1,0:T(8,128)}), f32[48,1024]{1,0:T(8,128)}) %reduce-scatter.9.cloned.1.call-update) | async-done | bytes 196624 | tf_op jit(solution)/shard_map/reduce_scatter | solution.py:44
  209.5 0.9 convert_element_type.71
  210.4 9.3 %all_gather.14 = bf16[48,4096]{1,0:T(8,128)(2,1)S(1)} all-gather(bf16[48,1024]{1,0:T(8,128)(2,1)S(1)} %convert_element_type.71), channel_id=1, replica_groups=mesh['src'=4,'dst'=8] {'src'}, dimensions={1}, use_global_device_ids=true | all-gather | bytes 491520 | tf_op jit(solution)/shard_map/all_gather | solution.py:47
  219.8 1.0 broadcast_in_dim.18
  220.8 3.5 %all-to-all-start.2 = ((bf16[48,8,1,1024]{3,0,2,1:T(8,128)(2,1)}), bf16[48,8,1,1024]{3,0,2,1:T(8,128)(2,1)S(1)}, u32[]{:S(2)}, u32[]{:S(2)}) async-start(bf16[48,8,1,1024]{3,0,2,1:T(8,128)(2,1)} %bitcast.53), calls=%async_computation.5 | async-start | bytes 1572864 | tf_op jit(solution)/shard_map/all_to_all | solution.py:52
  224.3 1.5 copy.16
  225.9 2.1 reshape.46
  228.0 17.2 %all-to-all-done.2 = bf16[48,8,1,1024]{3,0,2,1:T(8,128)(2,1)S(1)} async-done(((bf16[48,8,1,1024]{3,0,2,1:T(8,128)(2,1)}), bf16[48,8,1,1024]{3,0,2,1:T(8,128)(2,1)S(1)}, u32[]{:S(2)}, u32[]{:S(2)}) %all-to-all-start.2) | async-done | bytes 786464 | tf_op jit(solution)/shard_map/all_to_all | solution.py:52
  245.2 0.1 copy.20
  245.3 2.2 fusion.10
  247.5 6.9 %add_multiply_fusion = f32[2048,1024]{1,0:T(8,128)} fusion(f32[2048,1024]{1,0:T(8,128)S(1)} %fusion.10, bf16[8192,4096]{1,0:T(8,128)(2,1)} %param.6, bf16[48,8192]{1,0:T(8,128)(2,1)S(1)} %reshape.46, bf16[48,4096]{1,0:T(8,128)(2,1)S(1)} %fusion.2, f32[48]{0:T(128)S(1)} %copy-done.3), kind=kOutput, calls=%fused_computation | convolution fusion | flops 207765504 | bytes 21266944 | tf_op jit(solution)/shard_map/dot_general | solution.py:70
  (14 shorter events, 0.1 us)
Async XLA Ops:
  6.5 1.1 copy-start
  6.5 25.3 %copy-start.4 = (s32[48,4]{0,1:T(4,128)S(1)}, s32[48,4]{0,1:T(4,128)}, u32[]{:S(2)}) copy-start(s32[48,4]{0,1:T(4,128)} %param.8) | copy-start | bytes 2308
  6.5 25.4 %copy-start.2 = (bf16[48,4096]{1,0:T(8,128)(2,1)S(1)}, bf16[48,4096]{1,0:T(8,128)(2,1)}, u32[]{:S(2)}) copy-start(bf16[48,4096]{1,0:T(8,128)(2,1)} %param.10) | copy-start | bytes 1179652
  6.5 25.4 %copy-start.1 = (bf16[16,4096]{1,0:T(8,128)(2,1)S(1)}, bf16[16,4096]{1,0:T(8,128)(2,1)}, u32[]{:S(2)}) copy-start(bf16[16,4096]{1,0:T(8,128)(2,1)} %param.7) | copy-start | bytes 393220
  6.5 55.8 %reduce-scatter.5.cloned.1.call-start = ((), (), s32[]{:S(2)}) async-start(), calls=%async_computation.8 | async-start | bytes 491520 | tf_op jit(solution)/shard_map/reduce_scatter | solution.py:27
  31.8 70.3 %reduce-scatter.7.cloned.1.call-start = ((), (), s32[]{:S(2)}) async-start(), calls=%async_computation.9 | async-start | bytes 1769472 | tf_op jit(solution)/shard_map/reduce_scatter | solution.py:44
  85.8 15.1 %all-to-all-start = ((bf16[48,4,2,1,1024]{4,2,0,3,1:T(2,128)(2,1)}), bf16[48,4,2,1,1024]{4,2,0,3,1:T(2,128)(2,1)S(1)}, u32[]{:S(2)}, u32[]{:S(2)}) async-start(bf16[48,4,2,1,1024]{4,2,0,3,1:T(2,128)(2,1)} %copy.9), calls=%async_computation.1 | async-start | bytes 1572864 | tf_op jit(solution)/shard_map/all_to_all | solution.py:36
  114.0 28.3 %all-to-all-start.1 = ((bf16[48,8,1,1024]{3,0,2,1:T(8,128)(2,1)}), bf16[48,8,1,1024]{3,0,2,1:T(8,128)(2,1)S(1)}, u32[]{:S(2)}, u32[]{:S(2)}) async-start(bf16[48,8,1,1024]{3,0,2,1:T(8,128)(2,1)} %bitcast.6), calls=%async_computation.3 | async-start | bytes 1572864 | tf_op jit(solution)/shard_map/all_to_all | solution.py:52
  117.9 127.4 %copy-start.3 = (f32[48]{0:T(128)S(1)}, f32[48]{0:T(128)}, u32[]{:S(2)}) copy-start(f32[48]{0:T(128)} %param.11) | copy-start | bytes 580
  117.9 55.6 %reduce-scatter.11.cloned.1.call-start = ((), (), s32[]{:S(2)}) async-start(), calls=%async_computation.11 | async-start | bytes 491520 | tf_op jit(solution)/shard_map/reduce_scatter | solution.py:27
  142.1 67.4 %reduce-scatter.9.cloned.1.call-start = ((), (), s32[]{:S(2)}) async-start(), calls=%async_computation.10 | async-start | bytes 1769472 | tf_op jit(solution)/shard_map/reduce_scatter | solution.py:44
  196.7 23.1 %all-to-all-start.3 = ((bf16[48,4,2,1,1024]{4,2,0,3,1:T(2,128)(2,1)}), bf16[48,4,2,1,1024]{4,2,0,3,1:T(2,128)(2,1)S(1)}, u32[]{:S(2)}, u32[]{:S(2)}) async-start(bf16[48,4,2,1,1024]{4,2,0,3,1:T(2,128)(2,1)} %copy.15), calls=%async_computation.7 | async-start | bytes 1572864 | tf_op jit(solution)/shard_map/all_to_all | solution.py:36
  220.8 24.4 %all-to-all-start.2 = ((bf16[48,8,1,1024]{3,0,2,1:T(8,128)(2,1)}), bf16[48,8,1,1024]{3,0,2,1:T(8,128)(2,1)S(1)}, u32[]{:S(2)}, u32[]{:S(2)}) async-start(bf16[48,8,1,1024]{3,0,2,1:T(8,128)(2,1)} %bitcast.53), calls=%async_computation.5 | async-start | bytes 1572864 | tf_op jit(solution)/shard_map/all_to_all | solution.py:52
Sparse Core Ops, SparseCore 0:
  31.9 27.4 reduce-scatter.4
  62.1 38.2 reduce-scatter.6
  142.2 25.1 reduce-scatter.10
  172.4 37.0 reduce-scatter.8
where the time goes:
time: 262 us; the launch traced here: 261 us
  matrix products  119 us (45%)
  blocking collectives  59.9 us (23%)
  waiting for transfers between devices  38 us (15%)
  starting transfers between devices  15 us (6%)
  between operations  13.3 us (5%)
  local copies, waits for them, and re-layouts  12.1 us (5%)
  other arithmetic  3.8 us (1%)
    dot_general x2, matrix products, backward(): lax.dot_general(carried, transition, (((1,), (1,)), ((), ())), preferred_...  59.6 us
    dot_general x2, matrix products, forward(): jnp.dot(current, transition, preferred_element_type=jnp.float32)  48.3 us
    all_gather x2, blocking collectives, forward(): spread = lax.all_gather(advanced, 'dst', axis=1, tiled=True)  40.7 us
    all_gather x2, blocking collectives, backward(): spread = lax.all_gather(shared, 'src', axis=1, tiled=True)  19.2 us
    all_to_all x2, waiting for transfers between devices, backward(): lax.all_to_all(outgoing, 'dst', split_axis=1, concat_axis=2, tiled=True)  17.2 us
    all_to_all x2, waiting for transfers between devices, forward(): lax.all_to_all(shaped, 'src', split_axis=1, concat_axis=3, tiled=True)  11.3 us
    reduce_scatter x2, waiting for transfers between devices, backward(): lax.psum_scatter(partial_value, 'dst', scatter_dimension=1, tiled=True)  9.31 us
    dot_general x2, matrix products, per_device(): lax.dot_general(alpha_rows[:, :quarter_rows], weighted, (((0,), (0,)), ((...  9.17 us
  transfers between devices with their start and end apart: 8, of which 3 were waited for; matrix products, arithmetic and copies ran while one was open for 37% of the time, Pallas kernels for 0%

commit v1 on v0

--- a/solution.py
+++ b/solution.py
@@ -4,6 +4,16 @@
 from jax.sharding import PartitionSpec as P
 
 scaling = 0.75
+
+
+def turned_line(x, mesh_axis, along):
+    peers = lax.axis_size(mesh_axis)
+    held, tiles = (x, [x])
+    for _ in range(peers - 1):
+        held = lax.ppermute(held, mesh_axis, [(i, (i + 1) % peers) for i in range(peers)])
+        tiles.insert(0, held)
+    row_of_blocks = jnp.concatenate(tiles, axis=along)
+    return jnp.roll(row_of_blocks, (lax.axis_index(mesh_axis) + 1) * x.shape[along], axis=along)
 
 
 def per_device(transition, emit_cols, token_ids, alpha_start, beta_end, inverse_likelihood):
@@ -44,7 +54,7 @@
         shared = lax.psum_scatter(partial_value, "dst", scatter_dimension=1, tiled=True).astype(
             jnp.bfloat16
         )
-        spread = lax.all_gather(shared, "src", axis=1, tiled=True)
+        spread = turned_line(shared, "src", 1)
         tiles = spread.reshape(seq_rows, src_count, 1, slice_width)
         outgoing = jnp.broadcast_to(tiles, (seq_rows, src_count, tile_ratio, slice_width)).reshape(
             seq_rows, dst_count, 1, slice_width

time: 262 us -> 345 us (1.32)
  waiting for transfers between devices: 38 us -> 141 us
  blocking collectives: 59.9 us -> 30.9 us
  starting transfers between devices: 15 us -> 22.7 us
    reduce_scatter x2, waiting for transfers between devices: 0.02 us -> 48.3 us  [forward(): lax.psum_scatter(partial_value.astype(jnp.bfloat16), 'src', scatter_dimen...]
    reduce_scatter x2, waiting for transfers between devices: 9.31 us -> 46.7 us  [backward(): lax.psum_scatter(partial_value, 'dst', scatter_dimension=1, tiled=True)]
    ppermute x0 -> x6, waiting for transfers between devices: none -> 28.7 us  [turned_line(): lax.ppermute(held, mesh_axis, [(i, (i + 1) % peers) for i in range(peers)])]
    all_gather x2 -> x0, blocking collectives: 19.2 us -> none  [backward(): spread = lax.all_gather(shared, 'src', axis=1, tiled=True)]
    all_to_all x2, waiting for transfers between devices: 11.3 us -> 0.01 us  [forward(): lax.all_to_all(shaped, 'src', split_axis=1, concat_axis=3, tiled=True)]
    all_gather x2, blocking collectives: 40.7 us -> 30.9 us  [forward(): spread = lax.all_gather(advanced, 'dst', axis=1, tiled=True)]
    ppermute x0 -> x6, starting transfers between devices: none -> 6.91 us  [turned_line(): lax.ppermute(held, mesh_axis, [(i, (i + 1) % peers) for i in range(peers)])]
  transfers between devices with their start and end apart: 8 -> 14, of which waited for: 3 -> 9; matrix products, arithmetic and copies ran while one was open for 37% -> 27% of each run, Pallas kernels for 0% -> 0%
where the time goes in v1:
time: 345 us; the launch traced here: 344 us
  waiting for transfers between devices  141 us (41%)
  matrix products  117 us (34%)
  blocking collectives  30.9 us (9%)
  starting transfers between devices  22.7 us (7%)
  between operations  14.8 us (4%)
  local copies, waits for them, and re-layouts  11.8 us (3%)
  other arithmetic  6.1 us (2%)
    dot_general x2, matrix products, backward(): lax.dot_general(carried, transition, (((1,), (1,)), ((), ())), preferred_...  58.1 us
    dot_general x2, matrix products, forward(): jnp.dot(current, transition, preferred_element_type=jnp.float32)  48.7 us
    reduce_scatter x2, waiting for transfers between devices, forward(): lax.psum_scatter(partial_value.astype(jnp.bfloat16), 'src', scatter_dimen...  48.3 us
    reduce_scatter x2, waiting for transfers between devices, backward(): lax.psum_scatter(partial_value, 'dst', scatter_dimension=1, tiled=True)  46.7 us
    all_gather x2, blocking collectives, forward(): spread = lax.all_gather(advanced, 'dst', axis=1, tiled=True)  30.9 us
    ppermute x6, waiting for transfers between devices, turned_line(): lax.ppermute(held, mesh_axis, [(i, (i + 1) % peers) for i in range(peers)])  28.7 us
    all_to_all x2, waiting for transfers between devices, backward(): lax.all_to_all(outgoing, 'dst', split_axis=1, concat_axis=2, tiled=True)  17.3 us
    dot_general x2, matrix products, per_device(): lax.dot_general(alpha_rows[:, :quarter_rows], weighted, (((0,), (0,)), ((...  9.24 us
  transfers between devices with their start and end apart: 14, of which 9 were waited for; matrix products, arithmetic and copies ran while one was open for 27% of the time, Pallas kernels for 0%

profile of v1, /device:TPU:0, one launch (start us, length us, event | category | flops | bytes accessed | tf_op | source)
XLA Modules:
  0.0 344.4 jit_solution(3513803292428302613)
XLA Ops:
  7.4 0.8 slice_bitcast_fusion.1
  8.2 28.6 %fusion.4 = f32[48,8192]{1,0:T(8,128)} fusion(bf16[8192,4096]{1,0:T(8,128)(2,1)} %param.8, bf16[16,4096]{1,0:T(8,128)(2,1)} %param.9, bf16[48,4096]{1,0:T(8,128)(2,1)} %param.12, s32[48]{0:T(128)S(1)} %get-tuple-element.9), kind=kOutput, calls=%fused_computation.9 | convolution fusion | flops 3228304128 | bytes 69206208 | tf_op jit(solution)/shard_map/dot_general | solution.py:50
  36.8 37.0 %reduce-scatter.7.cloned.1.call-done = f32[48,1024]{1,0:T(8,128)} async-done(((f32[48,8192]{1,0:T(8,128)}), f32[48,1024]{1,0:T(8,128)}) %reduce-scatter.7.cloned.1.call-update) | async-done | bytes 196624 | tf_op jit(solution)/shard_map/reduce_scatter | solution.py:54
  73.8 0.9 convert_element_type.68
  74.8 1.7 collective-permute-start
  76.4 4.8 %collective-permute-done = bf16[48,1024]{1,0:T(8,128)(2,1)S(1)} collective-permute-done((bf16[48,1024]{1,0:T(8,128)(2,1)S(1)}, bf16[48,1024]{1,0:T(8,128)(2,1)S(1)}, u32[]{:S(2)}, u32[]{:S(2)}) %collective-permute-start) | collective-permute-done | bytes 98336 | tf_op jit(solution)/shard_map/ppermute | solution.py:13
  81.3 5.7 %collective-permute-done.1 = bf16[48,1024]{1,0:T(8,128)(2,1)S(1)} collective-permute-done((bf16[48,1024]{1,0:T(8,128)(2,1)S(1)}, bf16[48,1024]{1,0:T(8,128)(2,1)S(1)}, u32[]{:S(2)}, u32[]{:S(2)}) %collective-permute-start.1) | collective-permute-done | bytes 98336 | tf_op jit(solution)/shard_map/ppermute | solution.py:13
  87.0 5.5 %collective-permute-done.2 = bf16[48,1024]{1,0:T(8,128)(2,1)S(1)} collective-permute-done((bf16[48,1024]{1,0:T(8,128)(2,1)S(1)}, bf16[48,1024]{1,0:T(8,128)(2,1)S(1)}, u32[]{:S(2)}, u32[]{:S(2)}) %collective-permute-start.2) | collective-permute-done | bytes 98336 | tf_op jit(solution)/shard_map/ppermute | solution.py:13
  92.5 0.8 fusion.16
  93.4 1.0 broadcast_in_dim.16
  94.3 3.5 %all-to-all-start.1 = ((bf16[48,8,1,1024]{3,0,2,1:T(8,128)(2,1)}), bf16[48,8,1,1024]{3,0,2,1:T(8,128)(2,1)S(1)}, u32[]{:S(2)}, u32[]{:S(2)}) async-start(bf16[48,8,1,1024]{3,0,2,1:T(8,128)(2,1)} %bitcast.6), calls=%async_computation.3 | async-start | bytes 1572864 | tf_op jit(solution)/shard_map/all_to_all | solution.py:62
  98.0 24.2 %convolution_convert_fusion.1 = bf16[48,4096]{1,0:T(8,128)(2,1)} fusion(bf16[48,8192]{1,0:T(8,128)(2,1)S(1)} %copy-done, bf16[8192,4096]{1,0:T(8,128)(2,1)} %param.8), kind=kOutput, calls=%fused_computation.8 | convolution fusion | flops 3221422080 | bytes 68288512 | tf_op jit(solution)/shard_map/dot_general | solution.py:35
  122.2 0.3 fusion.32
  122.5 25.0 %reduce-scatter.5.cloned.1.call-done = bf16[48,1024]{1,0:T(8,128)(2,1)} async-done(((bf16[48,4096]{1,0:T(8,128)(2,1)}), bf16[48,1024]{1,0:T(8,128)(2,1)}) %reduce-scatter.5.cloned.1.call-update) | async-done | bytes 98320 | tf_op jit(solution)/shard_map/reduce_scatter | solution.py:37
  147.5 0.9 multiply_convert_fusion.3
  148.4 15.5 %all_gather.6 = bf16[48,8192]{1,0:T(8,128)(2,1)S(1)} all-gather(bf16[48,1024]{1,0:T(8,128)(2,1)S(1)} %multiply_convert_fusion.3), channel_id=1, replica_groups=mesh['src'=4,'dst'=8] {'dst'}, dimensions={1}, use_global_device_ids=true | all-gather | bytes 884736 | tf_op jit(solution)/shard_map/all_gather | solution.py:44
  163.9 0.6 reshape.39
  164.5 1.4 copy.15
  165.9 3.5 %all-to-all-start = ((bf16[48,4,2,1,1024]{4,2,0,3,1:T(2,128)(2,1)}), bf16[48,4,2,1,1024]{4,2,0,3,1:T(2,128)(2,1)S(1)}, u32[]{:S(2)}, u32[]{:S(2)}) async-start(bf16[48,4,2,1,1024]{4,2,0,3,1:T(2,128)(2,1)} %copy.15), calls=%async_computation.1 | async-start | bytes 1572864 | tf_op jit(solution)/shard_map/all_to_all | solution.py:46
  169.5 0.1 copy.25
  169.5 0.3 fusion.2
  169.9 29.6 %fusion.42 = f32[48,8192]{1,0:T(8,128)} fusion(bf16[48,4096]{1,0:T(8,128)(2,1)S(1)} %fusion.2, bf16[8192,4096]{1,0:T(8,128)(2,1)} %param.8), kind=kOutput, calls=%fused_computation.76 | convolution fusion | flops 3221225472 | bytes 69074944 | tf_op jit(solution)/shard_map/dot_general | solution.py:50
  199.5 0.2 reduce-scatter.11.cloned.1.call-start
  199.7 0.6 copy.16
  200.3 0.6 reshape.40
  200.9 24.6 %convolution_convert_fusion = bf16[48,4096]{1,0:T(8,128)(2,1)} fusion(bf16[48,8192]{1,0:T(8,128)(2,1)S(1)} %reshape.40, bf16[8192,4096]{1,0:T(8,128)(2,1)} %param.8), kind=kOutput, calls=%fused_computation.7 | convolution fusion | flops 3221422080 | bytes 68288512 | tf_op jit(solution)/shard_map/dot_general | solution.py:35
  225.5 0.3 fusion.33
  225.8 9.6 %reduce-scatter.9.cloned.1.call-done = f32[48,1024]{1,0:T(8,128)} async-done(((f32[48,8192]{1,0:T(8,128)}), f32[48,1024]{1,0:T(8,128)}) %reduce-scatter.9.cloned.1.call-update) | async-done | bytes 196624 | tf_op jit(solution)/shard_map/reduce_scatter | solution.py:54
  235.5 0.9 convert_element_type.71
  236.4 1.7 collective-permute-start.3
  238.1 23.2 %reduce-scatter.11.cloned.1.call-done = bf16[48,1024]{1,0:T(8,128)(2,1)} async-done(((bf16[48,4096]{1,0:T(8,128)(2,1)}), bf16[48,1024]{1,0:T(8,128)(2,1)}) %reduce-scatter.11.cloned.1.call-update) | async-done | bytes 98320 | tf_op jit(solution)/shard_map/reduce_scatter | solution.py:37
  261.4 0.9 multiply_convert_fusion.1
  262.3 1.5 collective-permute-start.4
  263.8 15.5 %all_gather.7 = bf16[48,8192]{1,0:T(8,128)(2,1)S(1)} all-gather(bf16[48,1024]{1,0:T(8,128)(2,1)S(1)} %multiply_convert_fusion.1), channel_id=1, replica_groups=mesh['src'=4,'dst'=8] {'dst'}, dimensions={1}, use_global_device_ids=true | all-gather | bytes 884736 | tf_op jit(solution)/shard_map/all_gather | solution.py:44
  279.3 0.6 reshape.45
  279.9 1.4 copy.21
  281.3 3.5 %all-to-all-start.3 = ((bf16[48,4,2,1,1024]{4,2,0,3,1:T(2,128)(2,1)}), bf16[48,4,2,1,1024]{4,2,0,3,1:T(2,128)(2,1)S(1)}, u32[]{:S(2)}, u32[]{:S(2)}) async-start(bf16[48,4,2,1,1024]{4,2,0,3,1:T(2,128)(2,1)} %copy.21), calls=%async_computation.7 | async-start | bytes 1572864 | tf_op jit(solution)/shard_map/all_to_all | solution.py:46
  284.8 2.0 collective-permute-start.5
  286.8 12.6 %collective-permute-done.5 = bf16[48,1024]{1,0:T(8,128)(2,1)S(1)} collective-permute-done((bf16[48,1024]{1,0:T(8,128)(2,1)}, bf16[48,1024]{1,0:T(8,128)(2,1)S(1)}, u32[]{:S(2)}, u32[]{:S(2)}) %collective-permute-start.5) | collective-permute-done | bytes 98336 | tf_op jit(solution)/shard_map/ppermute | solution.py:13
  299.4 1.6 fusion.9
  301.0 1.0 broadcast_in_dim.18
  302.0 5.0 %all-to-all-start.2 = ((bf16[48,8,1,1024]{3,0,2,1:T(8,128)(2,1)}), bf16[48,8,1,1024]{3,0,2,1:T(8,128)(2,1)S(1)}, u32[]{:S(2)}, u32[]{:S(2)}) async-start(bf16[48,8,1,1024]{3,0,2,1:T(8,128)(2,1)} %bitcast.53), calls=%async_computation.5 | async-start | bytes 1572864 | tf_op jit(solution)/shard_map/all_to_all | solution.py:62
  307.0 1.5 copy.22
  308.5 2.1 reshape.46
  310.6 17.3 %all-to-all-done.2 = bf16[48,8,1,1024]{3,0,2,1:T(8,128)(2,1)S(1)} async-done(((bf16[48,8,1,1024]{3,0,2,1:T(8,128)(2,1)}), bf16[48,8,1,1024]{3,0,2,1:T(8,128)(2,1)S(1)}, u32[]{:S(2)}, u32[]{:S(2)}) %all-to-all-start.2) | async-done | bytes 786464 | tf_op jit(solution)/shard_map/all_to_all | solution.py:62
  327.9 0.1 copy.26
  328.0 2.2 fusion.24
  330.2 7.0 %add_multiply_fusion = f32[2048,1024]{1,0:T(8,128)} fusion(f32[2048,1024]{1,0:T(8,128)S(1)} %fusion.24, bf16[8192,4096]{1,0:T(8,128)(2,1)} %param.8, bf16[48,8192]{1,0:T(8,128)(2,1)S(1)} %reshape.46, bf16[48,4096]{1,0:T(8,128)(2,1)} %copy-done.2, f32[48]{0:T(128)S(1)} %copy-done.4), kind=kOutput, calls=%fused_computation | convolution fusion | flops 207765504 | bytes 21266944 | tf_op jit(solution)/shard_map/dot_general | solution.py:80
  (26 shorter events, 0.2 us)
Async XLA Ops:
  7.4 90.6 %copy-start = (bf16[48,8192]{1,0:T(8,128)(2,1)S(1)}, bf16[48,8192]{1,0:T(8,128)(2,1)}, u32[]{:S(2)}) copy-start(bf16[48,8192]{1,0:T(8,128)(2,1)} %param.11) | copy-start | bytes 2359300
  7.4 66.5 %reduce-scatter.7.cloned.1.call-start = ((), (), s32[]{:S(2)}) async-start(), calls=%async_computation.9 | async-start | bytes 1769472 | tf_op jit(solution)/shard_map/reduce_scatter | solution.py:54
  8.2 113.9 %copy-start.1 = (bf16[16,4096]{1,0:T(8,128)(2,1)S(1)}, bf16[16,4096]{1,0:T(8,128)(2,1)}, u32[]{:S(2)}) copy-start(bf16[16,4096]{1,0:T(8,128)(2,1)} %param.9) | copy-start | bytes 393220
  74.8 6.5 %collective-permute-start = (bf16[48,1024]{1,0:T(8,128)(2,1)S(1)}, bf16[48,1024]{1,0:T(8,128)(2,1)S(1)}, u32[]{:S(2)}, u32[]{:S(2)}) collective-permute-start(bf16[48,1024]{1,0:T(8,128)(2,1)S(1)} %convert_element_type.68), channel_id=1, source_target_pairs={{0,8},{8,16},{16,24},{24,0},{1,9},{9,17},{17,25},{25,1},{2,10},{10... | collective-permute-start | bytes 294920 | tf_op jit(solution)/shard_map/ppermute | solution.py:13
  81.3 5.7 %collective-permute-start.1 = (bf16[48,1024]{1,0:T(8,128)(2,1)S(1)}, bf16[48,1024]{1,0:T(8,128)(2,1)S(1)}, u32[]{:S(2)}, u32[]{:S(2)}) collective-permute-start(bf16[48,1024]{1,0:T(8,128)(2,1)S(1)} %collective-permute-done), channel_id=1, source_target_pairs={{0,8},{8,16},{16,24},{24,0},{1,9},{9,17},{17,25},{25,1},{2,10},{10... | collective-permute-start | bytes 294920 | tf_op jit(solution)/shard_map/ppermute | solution.py:13
  87.0 5.5 %collective-permute-start.2 = (bf16[48,1024]{1,0:T(8,128)(2,1)S(1)}, bf16[48,1024]{1,0:T(8,128)(2,1)S(1)}, u32[]{:S(2)}, u32[]{:S(2)}) collective-permute-start(bf16[48,1024]{1,0:T(8,128)(2,1)S(1)} %collective-permute-done.1), channel_id=1, source_target_pairs={{0,8},{8,16},{16,24},{24,0},{1,9},{9,17},{17,25},{25,1},{2,10},{10... | collective-permute-start | bytes 294920 | tf_op jit(solution)/shard_map/ppermute | solution.py:13
  94.3 71.6 %all-to-all-start.1 = ((bf16[48,8,1,1024]{3,0,2,1:T(8,128)(2,1)}), bf16[48,8,1,1024]{3,0,2,1:T(8,128)(2,1)S(1)}, u32[]{:S(2)}, u32[]{:S(2)}) async-start(bf16[48,8,1,1024]{3,0,2,1:T(8,128)(2,1)} %bitcast.6), calls=%async_computation.3 | async-start | bytes 1572864 | tf_op jit(solution)/shard_map/all_to_all | solution.py:62
  97.9 49.6 %reduce-scatter.5.cloned.1.call-start = ((), (), s32[]{:S(2)}) async-start(), calls=%async_computation.8 | async-start | bytes 491520 | tf_op jit(solution)/shard_map/reduce_scatter | solution.py:37
  165.9 33.8 %all-to-all-start = ((bf16[48,4,2,1,1024]{4,2,0,3,1:T(2,128)(2,1)}), bf16[48,4,2,1,1024]{4,2,0,3,1:T(2,128)(2,1)S(1)}, u32[]{:S(2)}, u32[]{:S(2)}) async-start(bf16[48,4,2,1,1024]{4,2,0,3,1:T(2,128)(2,1)} %copy.15), calls=%async_computation.1 | async-start | bytes 1572864 | tf_op jit(solution)/shard_map/all_to_all | solution.py:46
  169.4 66.1 %reduce-scatter.9.cloned.1.call-start = ((), (), s32[]{:S(2)}) async-start(), calls=%async_computation.10 | async-start | bytes 1769472 | tf_op jit(solution)/shard_map/reduce_scatter | solution.py:54
  169.8 29.9 %copy-start.2 = (bf16[48,4096]{1,0:T(8,128)(2,1)}, bf16[48,4096]{1,0:T(8,128)(2,1)S(1)}, u32[]{:S(2)}) copy-start(bf16[48,4096]{1,0:T(8,128)(2,1)S(1)} %fusion.2) | copy-start | bytes 1179652
  169.9 158.1 %copy-start.4 = (f32[48]{0:T(128)S(1)}, f32[48]{0:T(128)}, u32[]{:S(2)}) copy-start(f32[48]{0:T(128)} %param.13) | copy-start | bytes 580
  199.5 61.9 %reduce-scatter.11.cloned.1.call-start = ((), (), s32[]{:S(2)}) async-start(), calls=%async_computation.11 | async-start | bytes 491520 | tf_op jit(solution)/shard_map/reduce_scatter | solution.py:37
  225.8 36.5 %copy-start.3 = (f32[48,4096]{1,0:T(8,128)}, f32[48,4096]{1,0:T(8,128)S(1)}, u32[]{:S(2)}) copy-start(f32[48,4096]{1,0:T(8,128)S(1)} %fusion.33) | copy-start | bytes 2359300
  236.4 25.9 %collective-permute-start.3 = (bf16[48,1024]{1,0:T(8,128)(2,1)S(1)}, bf16[48,1024]{1,0:T(8,128)(2,1)S(1)}, u32[]{:S(2)}, u32[]{:S(2)}) collective-permute-start(bf16[48,1024]{1,0:T(8,128)(2,1)S(1)} %convert_element_type.71), channel_id=1, source_target_pairs={{0,8},{8,16},{16,24},{24,0},{1,9},{9,17},{17,25},{25,1},{2,10},{10... | collective-permute-start | bytes 294920 | tf_op jit(solution)/shard_map/ppermute | solution.py:13
  262.3 22.5 %collective-permute-start.4 = (bf16[48,1024]{1,0:T(8,128)(2,1)S(1)}, bf16[48,1024]{1,0:T(8,128)(2,1)}, u32[]{:S(2)}, u32[]{:S(2)}) collective-permute-start(bf16[48,1024]{1,0:T(8,128)(2,1)S(1)} %collective-permute-done.3), channel_id=1, source_target_pairs={{0,8},{8,16},{16,24},{24,0},{1,9},{9,17},{17,25},{25,1},{2,10},{10... | collective-permute-start | bytes 294920 | tf_op jit(solution)/shard_map/ppermute | solution.py:13
  281.3 19.7 %all-to-all-start.3 = ((bf16[48,4,2,1,1024]{4,2,0,3,1:T(2,128)(2,1)}), bf16[48,4,2,1,1024]{4,2,0,3,1:T(2,128)(2,1)S(1)}, u32[]{:S(2)}, u32[]{:S(2)}) async-start(bf16[48,4,2,1,1024]{4,2,0,3,1:T(2,128)(2,1)} %copy.21), calls=%async_computation.7 | async-start | bytes 1572864 | tf_op jit(solution)/shard_map/all_to_all | solution.py:46
  284.8 14.6 %collective-permute-start.5 = (bf16[48,1024]{1,0:T(8,128)(2,1)}, bf16[48,1024]{1,0:T(8,128)(2,1)S(1)}, u32[]{:S(2)}, u32[]{:S(2)}) collective-permute-start(bf16[48,1024]{1,0:T(8,128)(2,1)} %collective-permute-done.4), channel_id=1, source_target_pairs={{0,8},{8,16},{16,24},{24,0},{1,9},{9,17},{17,25},{25,1},{2,10},{10... | collective-permute-start | bytes 294920 | tf_op jit(solution)/shard_map/ppermute | solution.py:13
  302.0 25.9 %all-to-all-start.2 = ((bf16[48,8,1,1024]{3,0,2,1:T(8,128)(2,1)}), bf16[48,8,1,1024]{3,0,2,1:T(8,128)(2,1)S(1)}, u32[]{:S(2)}, u32[]{:S(2)}) async-start(bf16[48,8,1,1024]{3,0,2,1:T(8,128)(2,1)} %bitcast.53), calls=%async_computation.5 | async-start | bytes 1572864 | tf_op jit(solution)/shard_map/all_to_all | solution.py:62
Sparse Core Ops, SparseCore 0:
  36.9 36.8 reduce-scatter.6
  199.6 35.8 reduce-scatter.8
  238.3 23.0 reduce-scatter.10
Sparse Core Ops, SparseCore 1:
  122.2 25.2 reduce-scatter.4
